TPU v7x, 512 devices: a whole 4x4x16 slice. The times are simulated.
512 devices in a mesh: branch: 2 (over core), tm: 32 (over z_lo, y), tok: 8 (over z_hi, x).
Axes of the slice: x: 4, y: 4, z: 16 (z_hi: 2, z_lo: 8; z = z_hi * 8 + z_lo), core: 2. Of those that a mesh axis runs over, the one named last changes fastest.
Arguments:
- states: float32 [32, 512, 3072], P('tm', 'tok'), may hold values from -6 to 6
- start_state: float32 [512, 3072], P('tok', 'branch'), may hold values from -12 to 12
- timesteps: int32 [32], P('tm'), may hold values from 0 to 49
- guidance_index: int32 [1], replicated, may hold values from 0 to 7
- modulation: float32 [2, 3, 3072], P('branch'), may hold values from -2.5 to 2.5
- w_query: bfloat16 [3072, 2048], P('branch', 'tok'), may hold values from -6 to 6, as said below
- w_key: bfloat16 [3072, 2048], P('branch', 'tok'), may hold values from -6 to 6, as said below
- w_value: bfloat16 [3072, 2048], P('branch', 'tok'), may hold values from -0.109375 to 0.109375
- w_out: bfloat16 [2048, 3072], P('tok', 'branch'), may hold values from -0.5 to 0.5
Outputs:
- updated_states: float32 [32, 512, 3072], P('tm', 'tok', 'branch')
Inputs may be any that keep to these rules, and one draw needn't show every extreme that they name: `w_query`: independent entries of mean zero. `w_key`: independent entries of mean zero.
All inputs are finite; a program needn't handle non-finite values.
Results may differ from a plain program's by a relative error of at most 0.0085.
The roundings to bfloat16 on the way count: a program that leaves them out, or rounds other values in their place, can miss the bound.
Values may be sent and summed in bfloat16 or wider, within the bound.
A program may use at most 64 MiB of HBM per device.

v0:
```python
import math

import jax
import jax.numpy as jnp
from jax import lax
from jax.sharding import Mesh
from jax.sharding import PartitionSpec as P

HD = 128
NSTEPS = 50
TOK = ("tok_0", "tok_1")


def swapped(x, axis, bit):
    return lax.ppermute(x, axis, [(i, i ^ 1 << bit) for i in range(lax.axis_size(axis))])


def in_order(blocks, dim):
    blocks = jnp.moveaxis(blocks, 0, dim)
    dims = blocks.shape
    return blocks.reshape(*dims[:dim], dims[dim] * dims[dim + 1], *dims[dim + 2 :])


def copy_for_each(x, axis):
    copies = jnp.broadcast_to(x, (lax.axis_size(axis), *x.shape))
    return lax.all_to_all(copies, axis, split_axis=0, concat_axis=0, tiled=True)


def gathered_copies(x, axis, dim):
    return in_order(copy_for_each(x, axis), dim)


def own_block(blocks, axes, sequence):
    inside = blocks.shape[1:]
    blocks = blocks.reshape(*(lax.axis_size(a) for a in axes), *inside)
    blocks = jnp.moveaxis(blocks, sequence, range(len(axes))).reshape(-1, *inside)
    for k in sequence:
        blocks = lax.psum_scatter(blocks, axes[k], scatter_dimension=0, tiled=True)
    return blocks[0]


def cut_along(x, dim, size):
    dims = x.shape
    blocks = x.reshape(*dims[:dim], size, dims[dim] // size, *dims[dim + 1 :])
    return jnp.moveaxis(blocks, dim, 0)


def sum_by_axis(x, axes, sequence, dim):
    size = lax.axis_size(axes)
    return own_block(cut_along(x, dim, size), axes, sequence)


def embed(step_ids, model_width):
    half_width = model_width // 2
    frequency = jnp.exp(-math.log(10000.0) * jnp.arange(half_width, dtype=jnp.float32) / half_width)
    phases = step_ids.astype(jnp.float32)[:, None] * frequency[None, :]
    return jnp.concatenate([jnp.sin(phases), jnp.cos(phases)], axis=1)


def body(
    states, start_state, timesteps, guidance_index, modulation, w_query, w_key, w_value, w_out
):
    tm_count, tok_count, model_width = states.shape
    half_width = model_width // 2
    branch_index = lax.axis_index("branch")
    modulation_row = modulation[0]
    embedding = embed(timesteps, model_width)
    mean_value = jnp.mean(states, axis=2, keepdims=True)
    centered = states - mean_value
    variance = jnp.mean(centered * centered, axis=2, keepdims=True)
    normed = centered / jnp.sqrt(variance + 1e-06)
    modulated = (
        normed * (1.0 + modulation_row[1]) + modulation_row[0] + embedding[:, None, :]
    ).astype(jnp.bfloat16)
    gathered = lax.all_gather(modulated, TOK, axis=1, tiled=True)
    lat_count = gathered.shape[1]
    flat_rows = gathered.reshape(tm_count * lat_count, model_width)
    col_count = w_query.shape[1]
    own_columns = lax.dynamic_slice_in_dim(flat_rows, branch_index * half_width, half_width, 1)
    partner_cols = lax.dynamic_slice_in_dim(
        flat_rows, (1 - branch_index) * half_width, half_width, 1
    )
    received = swapped(partner_cols, "branch", 0)
    for_partner = jnp.concatenate(
        [
            jnp.dot(received, w_query, preferred_element_type=jnp.float32),
            jnp.dot(received, w_key, preferred_element_type=jnp.float32),
            jnp.dot(received, w_value, preferred_element_type=jnp.float32),
        ],
        axis=1,
    )
    returned = swapped(for_partner, "branch", 0)
    query_full = (
        jnp.dot(own_columns, w_query, preferred_element_type=jnp.float32) + returned[:, :col_count]
    )
    key_full = (
        jnp.dot(own_columns, w_key, preferred_element_type=jnp.float32)
        + returned[:, col_count : 2 * col_count]
    )
    value_full = (
        jnp.dot(own_columns, w_value, preferred_element_type=jnp.float32)
        + returned[:, 2 * col_count :]
    )
    head_count = col_count // HD
    query_heads = query_full.astype(jnp.bfloat16).reshape(tm_count, lat_count, head_count, HD)
    key_heads = key_full.astype(jnp.bfloat16).reshape(tm_count, lat_count, head_count, HD)
    value_heads = value_full.astype(jnp.bfloat16).reshape(tm_count, lat_count, head_count, HD)
    scores = jnp.einsum(
        "tqhc,tkhc->thqk", query_heads, key_heads, preferred_element_type=jnp.float32
    ) * (1.0 / math.sqrt(HD))
    softmax_w = jax.nn.softmax(scores, axis=-1).astype(jnp.bfloat16)
    attended = jnp.einsum(
        "thqk,tkhc->qthc", softmax_w, value_heads, preferred_element_type=jnp.float32
    ).astype(jnp.bfloat16)
    attended = attended.reshape(lat_count, tm_count, col_count)
    out_full = gathered_copies(w_out, "branch", 1)
    summed = sum_by_axis(
        jnp.einsum("qtc,cd->qtd", attended, out_full, preferred_element_type=jnp.float32).astype(
            jnp.bfloat16
        ),
        TOK,
        (1, 0),
        0,
    ).astype(jnp.float32)
    drift = (1.0 + modulation_row[2]) * jnp.transpose(summed, (1, 0, 2))
    guide_scale = 1.5 + 0.5 * guidance_index[0].astype(jnp.float32)
    partner = swapped(drift, "branch", 0)
    conditional = jnp.where(branch_index == 0, drift, partner)
    unconditional = jnp.where(branch_index == 0, partner, drift)
    guided_full = unconditional + guide_scale * (conditional - unconditional)
    guided = lax.dynamic_slice_in_dim(guided_full, branch_index * half_width, half_width, 2)
    step_size = 2.0 * (1.0 + timesteps.astype(jnp.float32)) / NSTEPS
    increment = step_size[:, None, None] * guided
    local_prefix = jnp.cumsum(increment, axis=0)
    device_total = local_prefix[-1]
    column_blocks = lax.all_to_all(
        device_total[None, :, :], "tm", split_axis=2, concat_axis=0, tiled=True
    )
    running = jnp.cumsum(column_blocks, axis=0)
    exclusive = jnp.concatenate([jnp.zeros_like(running[:1]), running[:-1]], axis=0)
    earlier_sum = lax.all_to_all(exclusive, "tm", split_axis=0, concat_axis=2, tiled=True)[0]
    return start_state[None, :, :] + earlier_sum[None, :, :] + local_prefix


def solution(mesh):
    split = Mesh(
        mesh.devices.reshape(mesh.shape["branch"], mesh.shape["tm"], 2, 4),
        ("branch", "tm", "tok_0", "tok_1"),
    )
    placed = (
        P("tm", TOK, None),
        P(TOK, "branch"),
        P("tm"),
        P(),
        P("branch", None, None),
        P("branch", TOK),
        P("branch", TOK),
        P("branch", TOK),
        P(TOK, "branch"),
    )
    return jax.shard_map(
        body, mesh=split, in_specs=placed, out_specs=P("tm", TOK, "branch"), check_vma=False
    )
```

profile of v0, /device:TPU:2, one launch (start us, length us, event | category | flops | bytes accessed | tf_op | source)
XLA Modules:
  0.0 391.1 jit_solution(1131438883106606515)
XLA Ops:
  7.3 0.2 fusion.21
  7.5 0.8 slice_add_fusion.4
  8.3 1.3 reduce_sum.27
  9.6 1.4 multiply_reduce_fusion.1
  11.0 1.0 add_convert_fusion
  12.0 149.4 %all-gather.2.cloned.1.call-done = bf16[1,512,3072]{2,1,0:T(8,128)(2,1)} async-done(((bf16[1,64,3072]{2,1,0:T(8,128)(2,1)}), bf16[1,512,3072]{2,1,0:T(8,128)(2,1)}) %all-gather.2.cloned.1.call-update) | async-done | bytes 3145744 | tf_op jit(solution)/shard_map/all_gather | solution.py:75
  161.4 1.5 dynamic-slice_bitcast_fusion
  162.9 1.9 collective-permute-start
  164.8 3.4 collective-permute-done
  168.2 0.6 fusion.38
  168.9 0.6 fusion.39
  169.5 0.5 copy-done.4
  170.0 0.6 fusion.40
  170.6 1.3 pad_maximum_fusion
  171.9 2.0 collective-permute-start.1
  173.9 0.3 copy.25
  174.2 1.2 broadcast_in_dim.2
  175.5 3.7 all-to-all-start
  179.2 2.3 fusion.12
  181.5 0.2 copy-done.1
  181.7 2.4 fusion.13
  184.1 1.9 fusion.36
  186.0 2.8 fusion.14
  188.8 2.2 convolution_convert_fusion.1
  191.0 1.0 convolution_convert_fusion
  192.1 1.9 copy.26
  194.0 39.9 %reduce-scatter.3.cloned.1.call-done = bf16[2,64,1,3072]{3,1,2,0:T(8,128)(2,1)} async-done(((bf16[8,64,1,3072]{3,1,2,0:T(8,128)(2,1)}), bf16[2,64,1,3072]{3,1,2,0:T(8,128)(2,1)}) %reduce-scatter.3.cloned.1.call-update) | async-done | bytes 786448 | tf_op jit(solution)/shard_map/reduce_scatter | solution.py:38
  233.9 66.2 %reduce-scatter.5.cloned.1.call-done = bf16[1,64,1,3072]{3,1,2,0:T(8,128)(2,1)} async-done(((bf16[2,64,1,3072]{3,1,2,0:T(8,128)(2,1)}), bf16[1,64,1,3072]{3,1,2,0:T(8,128)(2,1)}) %reduce-scatter.5.cloned.1.call-update) | async-done | bytes 393232 | tf_op jit(solution)/shard_map/reduce_scatter | solution.py:38
  300.2 1.1 convert_multiply_fusion
  301.2 2.1 collective-permute-start.2
  304.0 1.4 collective-permute-done.2
  305.4 0.1 add_multiply_fusion
  305.5 0.5 copy.27
  306.0 0.5 broadcast.97
  306.5 7.2 %reduce.6 = f32[1536,64]{1,0:T(8,128)S(1)} reduce(f32[1536,1,64]{2,1,0:T(1,128)S(1)} %bitcast.78, f32[]{:T(128)} %broadcast.97), dimensions={1}, to_apply=%bitcast.52.reduce_sub_computation | reduce | bytes 786436
  313.7 0.5 reshape.177
  314.2 29.9 %all_to_all.41 = f32[32,1,3072]{2,1,0:T(1,128)S(1)} all-to-all(f32[32,1,3072]{2,1,0:T(1,128)S(1)} %reshape.177), channel_id=1, replica_groups=mesh['branch'=2,'tm'=32,'tok_0'=2,'tok_1'=4] {'tm'}, dimensions={0} | all-to-all | bytes 786432 | tf_op jit(solution)/shard_map/all_to_all | solution.py:136
  344.0 1.6 reduce.7
  345.6 1.0 reshape.178
  346.6 0.3 copy.29
  347.0 4.0 %fusion.37 = f32[32,64,48]{2,1,0:T(8,128)S(1)} fusion(f32[32,64,48]{2,1,0:T(8,128)S(1)} %copy.29), kind=kOutput, calls=%fused_computation.47 | output fusion | flops 3047424 | bytes 786432 | tf_op jit(solution)/shard_map/jit(cumsum)/reduce_window_sum | solution.py:139
  351.0 0.3 copy.38
  351.4 0.5 reshape.179
  351.9 29.8 %all_to_all.42 = f32[32,1,3072]{2,1,0:T(1,128)S(1)} all-to-all(f32[32,1,3072]{2,1,0:T(1,128)S(1)} %reshape.179), channel_id=1, replica_groups=mesh['branch'=2,'tm'=32,'tok_0'=2,'tok_1'=4] {'tm'}, dimensions={0} | all-to-all | bytes 786432 | tf_op jit(solution)/shard_map/all_to_all | solution.py:141
  381.7 1.6 reduce.8
  383.3 0.2 reshape.180
  383.5 0.2 copy.37
  383.8 0.8 bitcast_add_fusion
  (27 shorter events, 0.3 us)
Async XLA Ops:
  6.5 162.3 %copy-start = (bf16[1536,256]{1,0:T(8,128)(2,1)S(1)}, bf16[1536,256]{1,0:T(8,128)(2,1)}, u32[]{:S(2)}) copy-start(bf16[1536,256]{1,0:T(8,128)(2,1)} %param.15) | copy-start | bytes 2359300
  6.5 4.5 %copy-start.2 = (f32[1,64,3072]{2,1,0:T(8,128)S(1)}, f32[1,64,3072]{2,1,0:T(8,128)}, u32[]{:S(2)}) copy-start(f32[1,64,3072]{2,1,0:T(8,128)} %param.9) | copy-start | bytes 2359300
  6.5 154.9 %all-gather.2.cloned.1.call-start = ((), (), s32[]{:S(2)}) async-start(), calls=%async_computation.5 | async-start | bytes 3538944 | tf_op jit(solution)/shard_map/all_gather | solution.py:75
  12.0 156.2 %copy-start.3 = (bf16[1536,256]{1,0:T(8,128)(2,1)S(1)}, bf16[1536,256]{1,0:T(8,128)(2,1)}, u32[]{:S(2)}) copy-start(bf16[1536,256]{1,0:T(8,128)(2,1)} %param.14) | copy-start | bytes 2359300
  162.9 5.3 %collective-permute-start = (bf16[512,1536]{1,0:T(8,128)(2,1)S(1)}, bf16[512,1536]{1,0:T(8,128)(2,1)S(1)}, u32[]{:S(2)}, u32[]{:S(2)}) collective-permute-start(bf16[512,1536]{1,0:T(8,128)(2,1)S(1)} %dynamic-slice_bitcast_fusion), channel_id=1, source_target_pairs={{0,256},{256,0},{1,257},{257,1},{2,258},{258,2},{3,259},{259,3},{4... | collective-permute-start | bytes 4718600 | tf_op jit(solution)/shard_map/ppermute | solution.py:15
  168.9 1.1 copy-start.4
  170.6 3.3 copy-start.6
  171.9 7.3 %collective-permute-start.1 = (f32[512,768]{0,1:T(8,128)}, f32[512,768]{0,1:T(8,128)}, u32[]{:S(2)}, u32[]{:S(2)}) collective-permute-start(f32[512,768]{0,1:T(8,128)} %pad_maximum_fusion), channel_id=1, source_target_pairs={{0,256},{256,0},{1,257},{257,1},{2,258},{258,2},{3,259},{259,3},{4... | collective-permute-start | bytes 4718600 | tf_op jit(solution)/shard_map/ppermute | solution.py:15
  175.5 15.6 %all-to-all-start = ((bf16[2,256,1536]{1,2,0:T(8,128)(2,1)}), bf16[2,256,1536]{1,2,0:T(8,128)(2,1)S(1)}, u32[]{:S(2)}, u32[]{:S(2)}) async-start(bf16[2,256,1536]{1,2,0:T(8,128)(2,1)} %broadcast_in_dim.2), calls=%async_computation | async-start | bytes 3145728 | tf_op jit(solution)/shard_map/all_to_all | solution.py:26
  179.1 54.8 %reduce-scatter.3.cloned.1.call-start = ((), (), s32[]{:S(2)}) async-start(), calls=%async_computation.6 | async-start | bytes 3932160 | tf_op jit(solution)/shard_map/reduce_scatter | solution.py:38
  179.2 2.5 copy-start.1
  184.1 1.9 copy-start.5
  194.0 106.2 %reduce-scatter.5.cloned.1.call-start = ((), (), s32[]{:S(2)}) async-start(), calls=%async_computation.7 | async-start | bytes 1179648 | tf_op jit(solution)/shard_map/reduce_scatter | solution.py:38
  301.2 4.2 %collective-permute-start.2 = (f32[1,64,3072]{2,1,0:T(8,128)S(1)}, f32[1,64,3072]{2,1,0:T(8,128)S(1)}, u32[]{:S(2)}, u32[]{:S(2)}) collective-permute-start(f32[1,64,3072]{2,1,0:T(8,128)S(1)} %convert_multiply_fusion), channel_id=1, source_target_pairs={{0,256},{256,0},{1,257},{257,1},{2,258},{258,2},{3,259},{259,3},{4... | collective-permute-start | bytes 2359304 | tf_op jit(solution)/shard_map/ppermute | solution.py:15
  381.7 2.1 copy-start.7
Sparse Core Ops, SparseCore 0:
  12.1 149.2 all-gather.1
  194.1 39.7 reduce-scatter.2
  236.7 63.4 reduce-scatter.4
where the time goes:
time: 392 us; the launch traced here: 391 us
  waiting for transfers between devices  260 us (66%)
  blocking collectives  59.6 us (15%)
  other arithmetic  22.2 us (6%)
  between operations  14.9 us (4%)
  matrix products  14.5 us (4%)
  local copies, waits for them, and re-layouts  9.82 us (3%)
  starting transfers between devices  9.81 us (3%)
    all_gather x1, waiting for transfers between devices, body(): gathered = lax.all_gather(modulated, TOK, axis=1, tiled=True)  149 us
    reduce_scatter x2, waiting for transfers between devices, own_block(): blocks = lax.psum_scatter(blocks, axes[k], scatter_dimension=0, tiled=True)  106 us
    all_to_all x1, blocking collectives, body(): lax.all_to_all(device_total[None, :, :], 'tm', split_axis=2, concat_axis=...  29.9 us
    all_to_all x1, blocking collectives, body(): lax.all_to_all(exclusive, 'tm', split_axis=0, concat_axis=2, tiled=True)[0]  29.8 us
  transfers between devices with their start and end apart: 7, of which 5 were waited for; matrix products, arithmetic and copies ran while one was open for 3% of the time, Pallas kernels for 0%

commit v1 on v0

v1 whole, which is shorter than its diff:
```python
import functools
import math

import jax
import jax.numpy as jnp
from jax import lax
from jax.experimental import pallas as pl
from jax.experimental.pallas import tpu as pltpu
from jax.sharding import Mesh
from jax.sharding import PartitionSpec as P

HD = 128
NSTEPS = 50
BF = jnp.bfloat16
F32 = jnp.float32
AXES = ("b", "l", "y", "h", "x")


def embed(step_ids, model_width):
    half_width = model_width // 2
    frequency = jnp.exp(-math.log(10000.0) * jnp.arange(half_width, dtype=F32) / half_width)
    phases = step_ids.astype(F32)[:, None] * frequency[None, :]
    return jnp.concatenate([jnp.sin(phases), jnp.cos(phases)], axis=1)


def remote(src, dst, send_sem, recv_sem, device):
    return pltpu.make_async_remote_copy(
        src_ref=src,
        dst_ref=dst,
        send_sem=send_sem,
        recv_sem=recv_sem,
        device_id=device,
        device_id_type=pl.DeviceIdType.MESH,
    )


def kernel(
    nl, ny, nx, index,
    states, start, mod, emb, misc, w_query, w_key, w_value, w_out, out,
    xs, gathered, wq, qkv, att, relay, full, wo, acc, pre, ob, st, eb, sb, mp, ms, loc, ss, rs,
):
    b, l, y, h, x = (lax.axis_index(a) for a in AXES)
    rows, width = xs.shape
    half = width // 2
    quarter = half // ny
    cols = w_out.shape[0]
    head_count = cols // HD
    side_rows = nx * rows
    me = h * nx + x
    far = 1 - h
    other = far * nx + x
    opposite = {"h": far}
    partner = {"b": 1 - b}
    xto = [{"x": lax.rem(x + d, nx)} for d in range(nx)]
    xfrom = [lax.rem(x + nx - d, nx) for d in range(nx)]
    yto = [{"y": lax.rem(y + d, ny)} for d in range(ny)]
    yfrom = [lax.rem(y + ny - d, ny) for d in range(ny)]
    up = {"l": lax.rem(l + 1, nl), "h": jnp.where(l == nl - 1, far, h)}
    down = {"l": lax.rem(l + nl - 1, nl), "h": jnp.where(l == 0, far, h)}
    sent = []

    def sem(name):
        return index.setdefault(name, len(index))

    def send(name, src, dst, device):
        copy = remote(src, dst, ss.at[sem(name)], rs.at[sem(name)], device)
        copy.start()
        sent.append(copy)

    def arrived(name, dst):
        remote(dst, dst, ss.at[sem(name)], rs.at[sem(name)], partner).wait_recv()

    own_rows = pl.ds(pl.multiple_of(b * half, half), half)
    their_rows = pl.ds(pl.multiple_of((1 - b) * half, half), half)
    own_cols = pl.ds(pl.multiple_of(y * quarter, quarter), quarter)

    load = pltpu.make_async_copy(states.at[0], xs, loc.at[0])
    load.start()
    barrier = pltpu.get_barrier_semaphore()
    peers = [opposite, partner, up, down] + xto[1:] + yto[1:]
    for peer in peers:
        pl.semaphore_signal(barrier, inc=1, device_id=peer, device_id_type=pl.DeviceIdType.MESH)
    local = []
    for j, w in enumerate((w_query, w_key, w_value)):
        local.append(pltpu.make_async_copy(w, wq.at[j, own_rows], loc.at[1 + j]))
    local.append(pltpu.make_async_copy(start.at[:, own_cols], st, loc.at[4]))
    local.append(pltpu.make_async_copy(w_out.at[:, own_cols], wo.at[me], loc.at[5]))
    for copy in local:
        copy.start()
    ms[y] = misc[...]
    load.wait()

    @pl.loop(0, rows // 16)
    def _(r):
        at = pl.ds(pl.multiple_of(r * 16, 16), 16)
        value = xs[at, :]
        centered = value - jnp.mean(value, axis=1, keepdims=True)
        variance = jnp.mean(centered * centered, axis=1, keepdims=True)
        normed = centered / jnp.sqrt(variance + 1e-06)
        value = normed * (1.0 + mod[0, 1:2, :]) + mod[0, 0:1, :] + emb[...]
        gathered[me, at, :] = value.astype(BF)

    pl.semaphore_wait(barrier, len(peers))

    chunks = rows // 16
    for c in range(chunks):
        block = gathered.at[me, pl.ds(c * 16, 16)]
        send(("nz", c), block, block, opposite)
    for d in range(1, nx):
        send(("nx", d), gathered.at[me], gathered.at[me], xto[d])
    for j, w in enumerate((w_query, w_key, w_value)):
        send(("w", j), w, wq.at[j, own_rows], partner)
    send("mod", mod, mp, partner)
    for d in range(1, ny):
        send(("misc", d), misc, ms.at[y], yto[d])
    for copy in local:
        copy.wait()

    points = nl // 2
    distance = jnp.minimum(l, nl - 1 - l)
    inward = {"l": jnp.where(l < points, l + 1, l - 1)}
    edge = remote(
        wo.at[me], wo.at[me], ss.at[sem("edge")], rs.at[sem("chain")], {"l": nl - 1 - l, "h": far}
    )
    hop = remote(wo.at[other], wo.at[other], ss.at[sem("hop")], rs.at[sem("chain")], inward)
    pl.when(distance == 0)(edge.start)

    def chain_point(p):
        @pl.when(distance == p)
        def _():
            arrived("chain", wo.at[other])
            if p + 1 < points:
                hop.start()

    def project(side):
        to = pl.ds(pl.multiple_of(side * side_rows, side_rows), side_rows)

        @pl.loop(0, 3)
        def _(j):
            block = gathered[pl.ds(side * nx, nx)].reshape(side_rows, width)
            qkv[j, to, :] = jnp.dot(block, wq[j], preferred_element_type=F32).astype(BF)

    for j in range(3):
        arrived(("w", j), wq.at[j, their_rows])
    arrived("mod", mp)
    for d in range(1, nx):
        arrived(("nx", d), gathered.at[h * nx + xfrom[d]])

    def pass_on(c):
        block = gathered.at[other, pl.ds(c * 16, 16)]
        arrived(("nz", c), block)
        for d in range(1, nx):
            send(("nf", d, c), block, block, xto[d])

    pass_on(0)
    project(h)
    chain_point(0)
    for c in range(1, chunks):
        pass_on(c)
    for d in range(1, nx):
        send(("wx", d), wo.at[me], wo.at[me], xto[d])
    for p in range(1, points - 1):
        chain_point(p)
    for c in range(chunks):
        for d in range(1, nx):
            arrived(("nf", d, c), gathered.at[far * nx + xfrom[d], pl.ds(c * 16, 16)])
    project(far)

    def attend(side):
        to = pl.ds(pl.multiple_of(side * side_rows, side_rows), side_rows)
        for k in range(head_count):
            at = pl.ds(k * HD, HD)
            scores = lax.dot_general(
                qkv[0, to, at], qkv[1, :, at], (((1,), (1,)), ((), ())), preferred_element_type=F32
            ) * (1.0 / math.sqrt(HD))
            weight = jnp.exp(scores - jnp.max(scores, axis=1, keepdims=True))
            weight = weight / jnp.sum(weight, axis=1, keepdims=True)
            result = jnp.dot(weight.astype(BF), qkv[2, :, at], preferred_element_type=F32)
            att[pl.ds(side * nx, nx), :, at] = result.astype(BF).reshape(nx, rows, HD)

    order = list(range(1, nx)) + [0]
    attend(far)
    for d in order:
        send(("az", d), att.at[far * nx + lax.rem(x + d, nx)], relay.at[d], opposite)
    attend(h)
    for d in range(1, nx):
        send(("ax", 0, d), att.at[h * nx + lax.rem(x + d, nx)], full.at[me, y, b], xto[d])
    keep = pltpu.make_async_copy(att.at[me], full.at[me, y, b], loc.at[6])
    keep.start()
    keep.wait()

    def spread(side, part, d):
        block = full.at[side * nx + xfrom[d], y, b]
        if d:
            arrived(("ax", part, d), block)
        for e in range(1, ny):
            send(("ay", part, e, d), block, block, yto[e])

    def swap(side, part, e):
        blocks = full.at[pl.ds(side * nx, nx), yfrom[e], b]
        send(("ac", part, e), blocks, blocks, partner)

    def collect(side, part):
        for e in range(1, ny):
            for d in range(nx):
                arrived(("ay", part, e, d), full.at[side * nx + xfrom[d], yfrom[e], b])
            swap(side, part, e)

    def finish(side, part):
        for e in range(ny):
            arrived(("ac", part, e), full.at[pl.ds(side * nx, nx), yfrom[e], 1 - b])

    def multiply(side, first):
        for i in range(nx):
            group = side * nx + i
            block = full[group].reshape(ny * 2 * rows, cols)
            term = jnp.dot(block, wo[group], preferred_element_type=F32).astype(BF).astype(F32)
            if first and i == 0:
                acc[...] = term
            else:
                acc[...] += term

    for d in range(nx):
        spread(h, 0, d)
    swap(h, 0, 0)
    chain_point(points - 1)
    for d in range(1, nx):
        send(("wf", d), wo.at[other], wo.at[other], xto[d])
    collect(h, 0)

    for d in order:
        arrived(("az", d), relay.at[d])
        if d:
            send(("ax", 1, d), relay.at[d], full.at[other, y, b], xto[d])
        else:
            take = pltpu.make_async_copy(relay.at[0], full.at[other, y, b], loc.at[7])
            take.start()
            take.wait()
    for d in range(nx):
        spread(far, 1, d)
    swap(far, 1, 0)
    for d in range(1, nx):
        arrived(("wx", d), wo.at[h * nx + xfrom[d]])
    finish(h, 0)
    multiply(h, True)
    collect(far, 1)
    for d in range(1, nx):
        arrived(("wf", d), wo.at[far * nx + xfrom[d]])
    for e in range(1, ny):
        arrived(("misc", e), ms.at[yfrom[e]])
    finish(far, 1)
    multiply(far, False)

    channels = pl.ds(pl.multiple_of(b * half + y * quarter, quarter), quarter)
    own_gate = 1.0 + mod[0, 2:3, channels]
    their_gate = 1.0 + mp[0, 2:3, channels]
    gate_cond = jnp.where(b == 0, own_gate, their_gate)
    gate_free = jnp.where(b == 0, their_gate, own_gate)
    scale = misc[1:2, :]
    for i in range(ny):
        cond = gate_cond * acc[pl.ds(2 * i * rows, rows), :]
        free = gate_free * acc[pl.ds((2 * i + 1) * rows, rows), :]
        step = ms[i, 0:1, :] * (free + scale * (cond - free))
        pre[i] = step if i == 0 else pre[i - 1] + step

    @pl.when(l == 0)
    def _():
        eb[...] = jnp.zeros_like(eb)

    size = 16
    pieces = rows // size
    links = []
    for c in range(pieces):
        at = pl.ds(c * size, size)
        link = remote(
            sb.at[at], eb.at[at], ss.at[sem(("e", c))], rs.at[sem(("e", c))], {"l": lax.rem(l + 1, nl)}
        )
        links.append(link)

        @pl.when(l > 0)
        def _(at=at, c=c):
            arrived(("e", c), eb.at[at])

        @pl.when(l < nl - 1)
        def _(at=at, link=link):
            sb[at, :] = eb[at, :] + pre[ny - 1, at, :]
            link.start()

        base = st[at, :] + eb[at, :]
        for e in range(1, ny):
            ob[e, at, :] = base + pre[lax.rem(y + e, ny), at, :]
            send(("o", e, c), ob.at[e, at], out.at[0, at, own_cols], yto[e])
        out[0, at, own_cols] = base + pre[y, at, :]
    for c in range(pieces):
        for e in range(1, ny):
            columns = pl.ds(pl.multiple_of(yfrom[e] * quarter, quarter), quarter)
            arrived(("o", e, c), out.at[0, pl.ds(c * size, size), columns])

    for copy in sent:
        copy.wait_send()
    pl.when(distance == 0)(edge.wait_send)
    if points > 1:
        pl.when(distance < points - 1)(hop.wait_send)

    @pl.when(l < nl - 1)
    def _():
        for link in links:
            link.wait_send()


def body(nl, ny, nx, states, start, timesteps, guidance, modulation, w_query, w_key, w_value, w_out):
    _, rows, width = states.shape
    half = width // 2
    quarter = half // ny
    cols = w_out.shape[0]
    blocks = 2 * nx
    step = 2.0 * (1.0 + timesteps.astype(F32)) / NSTEPS
    scale = 1.5 + 0.5 * guidance.astype(F32)
    line = lax.broadcasted_iota(jnp.int32, (8, quarter), 0)
    misc = jnp.where(line == 0, step[0], scale[0])
    hbm = pl.BlockSpec(memory_space=pl.ANY)
    vmem = pl.BlockSpec(memory_space=pltpu.VMEM)
    return pl.pallas_call(
        functools.partial(kernel, nl, ny, nx, {}),
        out_shape=jax.ShapeDtypeStruct((1, rows, half), F32),
        in_specs=[hbm, hbm, vmem, vmem, vmem, hbm, hbm, hbm, hbm],
        out_specs=vmem,
        scratch_shapes=[
            pltpu.VMEM((rows, width), F32),
            pltpu.VMEM((blocks, rows, width), BF),
            pltpu.VMEM((3, width, cols), BF),
            pltpu.VMEM((3, blocks * rows, cols), BF),
            pltpu.VMEM((blocks, rows, cols), BF),
            pltpu.VMEM((nx, rows, cols), BF),
            pltpu.VMEM((blocks, ny, 2, rows, cols), BF),
            pltpu.VMEM((blocks, cols, quarter), BF),
            pltpu.VMEM((ny * 2 * rows, quarter), F32),
            pltpu.VMEM((ny, rows, quarter), F32),
            pltpu.VMEM((ny, rows, quarter), F32),
            pltpu.VMEM((rows, quarter), F32),
            pltpu.VMEM((rows, quarter), F32),
            pltpu.VMEM((rows, quarter), F32),
            pltpu.VMEM((1, 3, width), F32),
            pltpu.VMEM((ny, 8, quarter), F32),
            pltpu.SemaphoreType.DMA((8,)),
            pltpu.SemaphoreType.DMA((128,)),
            pltpu.SemaphoreType.DMA((128,)),
        ],
        compiler_params=pltpu.CompilerParams(
            collective_id=0, has_side_effects=True, vmem_limit_bytes=48 << 20
        ),
        name="picard",
    )(states, start, modulation, embed(timesteps, width), misc, w_query, w_key, w_value, w_out)


def build(fine, nl, ny, nx):
    tok = ("h", "x")
    tm = ("l", "y")
    placed = (
        P(tm, tok, None),
        P(tok, "b"),
        P(tm),
        P(),
        P("b", None, None),
        P("b", tok),
        P("b", tok),
        P("b", tok),
        P(tok, "b"),
    )
    return jax.shard_map(
        functools.partial(body, nl, ny, nx),
        mesh=fine,
        in_specs=placed,
        out_specs=P(tm, tok, "b"),
        check_vma=False,
    )


def solution(mesh):
    nl, ny, nx = 8, 4, 4
    return build(Mesh(mesh.devices.reshape(2, nl, ny, 2, nx), AXES), nl, ny, nx)
```

time: 392 us -> 129 us (0.33)
  the two profiles are of different devices: /device:TPU:2 before, /device:TPU:224 now
where the time goes in v1:
time: 129 us
  Pallas kernels  120 us (93%)
  local copies, waits for them, and re-layouts  7.49 us (6%)
  between operations  1.37 us (1%)
    pallas_call x1, Pallas kernels, body(): pl.pallas_call(functools.partial(kernel, nl, ny, nx, {}), out_shape=jax.S...  120 us
    unnamed x16, local copies, waits for them, and re-layouts  7.42 us

profile of v1, /device:TPU:224, one launch (start us, length us, event | category | flops | bytes accessed | tf_op | source)
XLA Modules:
  0.0 128.7 jit_solution(5906781021530452467)
XLA Ops:
  0.7 0.0 copy-start.6
  1.3 0.1 iota.13.misc
  1.4 0.2 fusion
  1.6 0.0 copy-done.6
  1.7 0.0 copy-start
  1.7 1.1 copy-done
  2.8 0.0 copy-start.1
  2.8 1.1 copy-done.1
  3.9 0.0 copy-start.2
  3.9 1.1 copy-done.2
  5.1 0.0 copy-start.3
  5.1 1.1 copy-done.3
  6.2 0.0 copy-start.4
  6.2 1.1 copy-done.4
  7.3 0.0 copy-start.5
  7.3 1.0 copy-done.5
  8.3 119.6 %picard.1 = f32[1,64,1536]{2,1,0:T(8,128)S(1)} custom-call(f32[1,64,3072]{2,1,0:T(8,128)S(1)} %copy-done, f32[64,1536]{1,0:T(8,128)S(1)} %copy-done.5, f32[1,3,3072]{2,1,0:T(4,128)S(1)} %copy.10.mod, f32[1,3072]{1,0:T(1,128)S(1)} %pad_maximum_fusion.emb, f32[8,384]{1,0:T(8,128)S(1)} %iota.13.misc, bf16[1536,256]{1,0:T(8,128)(2,1)S(1)} %copy-done.1, ...), custom_call_target="tpu_custom_call" | custom-call | tf_op jit(solution)/shard_map/picard/pallas_call | solution.py:323
  128.0 0.7 copy.14
  (3 shorter events, 0.0 us)
Async XLA Ops:
  0.7 1.0 copy-start.6
  1.7 1.1 copy-start
  2.8 1.1 copy-start.1
  3.9 1.1 copy-start.2
  5.1 1.1 copy-start.3
  6.2 1.1 copy-start.4
  7.3 1.0 copy-start.5
